TPU v7x, 32 devices: a whole 2x2x4 slice. The times are simulated.
32 devices in a mesh: groups: 2 (over y), ctx: 8 (over z, x), head: 2 (over core).
Axes of the slice: x: 2, y: 2, z: 4, core: 2. Of those that a mesh axis runs over, the one named last changes fastest.
Arguments:
- queries: bfloat16 [2048, 2048], P(('groups', 'ctx'), 'head'), parts along dimension 0, may hold values from -80 to 80
- keys: bfloat16 [2048, 512], P(('groups', 'ctx'), 'head'), parts along dimension 0, may hold values from -6 to 6
- values: bfloat16 [2048, 512], P(('groups', 'ctx'), 'head'), parts along dimension 0, may hold values from -6 to 6
- pattern: int32 [16, 8], P(('groups', 'ctx')), parts along dimension 0, may hold values from -1 to 7, as said below
- x_in: bfloat16 [2048, 1024], P(('groups', 'ctx'), 'head'), parts along dimension 0, may hold values from -2 to 2
- z_gate: bfloat16 [2048, 1024], P(('groups', 'ctx'), 'head'), parts along dimension 0, may hold values from -6 to 6
- bmat: bfloat16 [2048, 256], P(('groups', 'ctx'), 'head'), parts along dimension 0, may hold values from -6 to 6
- cmat: bfloat16 [2048, 256], P(('groups', 'ctx'), 'head'), parts along dimension 0, may hold values from -0.5 to 0.5
- log_decay: float32 [32, 1024], P(('groups', 'head'), 'ctx'), parts along dimension 0, may hold values from -2 to 0
- gain: float32 [1024], P('head'), may hold values from 0.1 to 1.9
Outputs:
- attn_out: bfloat16 [2048, 2048], P(('groups', 'ctx'), 'head'), parts along dimension 0
- ssm_out: bfloat16 [2048, 1024], P(('groups', 'ctx'), 'head'), parts along dimension 0
There are 2 independent parts, one for each index of `groups`. A program takes and returns all parts, laid end to end along the dimension named above; an argument that names none is the same for every part. Nothing has to cross between parts.
Inputs may be any that keep to these rules, and one draw needn't show every extreme that they name: `pattern`: entry 0 of row q is q; the other entries are distinct blocks from q - 3 to q - 1, or -1 where no block is listed.
All inputs are finite; a program needn't handle non-finite values.
Results may differ from a plain program's by a relative error of at most 0.009.
Values may be sent and summed in bfloat16 or wider, within the bound.
No kernel may reach another device: no remote copies, remote signals or barrier semaphores. Data moves between devices by JAX's collectives and lax.ppermute only.
A program may use at most 128 MiB of HBM per device.

v0:
```python
import jax
import jax.numpy as jnp
from jax import lax
from jax.sharding import PartitionSpec as P

BLK = 128
SCAN_BLK = 128
HD = 128
P_SIZE = 64
N = 128
KSEL = 8
REACH = 3


def entering(shard, axis, combine, identity):
    peers, index = (lax.axis_size(axis), lax.axis_index(axis))
    everything = jax.tree.map(lambda part: lax.all_gather(part, axis), shard)
    start = jax.tree.map(
        lambda part, zero: jnp.broadcast_to(jnp.asarray(zero, part.dtype), part.shape),
        shard,
        identity,
    )

    def step(k, before):
        reached = k < index
        new = combine(before, jax.tree.map(lambda part: part[k], everything))
        return jax.tree.map(lambda a, b: jnp.where(reached, a, b), new, before)

    return lax.fori_loop(0, peers, step, start)


def passed_along(value, axis, steps):
    count = lax.axis_size(axis)
    initial, last = (max(0, -steps), min(count, count - steps))
    return lax.ppermute(value, axis, [(source, source + steps) for source in range(initial, last)])


def combine_states(earlier, later):
    return (earlier[0] + later[0], jnp.exp(later[0])[..., None, None] * earlier[1] + later[1])


def split_parts(multiplier):
    upper = multiplier.astype(jnp.bfloat16)
    lower = (multiplier - upper.astype(jnp.float32)).astype(jnp.bfloat16)
    return (upper, lower)


def two_pass(form, multiplier, other):
    upper, lower = split_parts(multiplier)
    first = jnp.einsum(form, upper, other, preferred_element_type=jnp.float32)
    return first + jnp.einsum(form, lower, other, preferred_element_type=jnp.float32)


def double_sweep_right(form, other, multiplier):
    upper, lower = split_parts(multiplier)
    first = jnp.einsum(form, other, upper, preferred_element_type=jnp.float32)
    return first + jnp.einsum(form, other, lower, preferred_element_type=jnp.float32)


def mamba_mixer(x_in, z_gate, bmat, cmat, log_decay, gain, length):
    total_len = x_in.shape[0]
    heads_here = log_decay.shape[0]
    groups_here = bmat.shape[1] // N
    per_group = heads_here // groups_here
    block_count = total_len // length
    x_half = x_in.reshape(block_count, length, groups_here, per_group, P_SIZE)
    b_half = bmat.reshape(block_count, length, groups_here, N)
    c_half = cmat.reshape(block_count, length, groups_here, N)
    log_rates = log_decay.reshape(groups_here, per_group, block_count, length)
    cumulative = jnp.cumsum(log_rates, axis=3)
    spread = cumulative[..., :, None] - cumulative[..., None, :]
    lower_tri = jnp.tril(jnp.ones((length, length), dtype=bool))
    decays = jnp.exp(jnp.where(lower_tri, spread, -jnp.inf))
    affinity = jnp.einsum("clgn,cmgn->cglm", c_half, b_half, preferred_element_type=jnp.float32)
    mixing = affinity[:, :, None] * jnp.transpose(decays, (2, 0, 1, 3, 4))
    inside = two_pass("cghlm,cmghp->clghp", mixing, x_half)
    weights = jnp.exp(cumulative[..., -1:] - cumulative)
    weighted = x_half.astype(jnp.float32) * jnp.transpose(weights, (2, 3, 0, 1))[..., None]
    summary = two_pass("clghp,clgn->cghpn", weighted, b_half)
    block_decay = cumulative[..., -1]
    running = jnp.zeros((groups_here, per_group, P_SIZE, N), jnp.float32)
    decay_sum = jnp.zeros((groups_here, per_group), jnp.float32)
    starts = running
    prefixes = decay_sum
    running = jnp.exp(block_decay[..., 0])[..., None, None] * running + summary[0]
    decay_sum = block_decay[..., 0]
    identity = (jnp.zeros_like(decay_sum), jnp.zeros_like(running))
    incoming = entering((decay_sum, running), "ctx", combine_states, identity)
    entry = jnp.stack([starts + jnp.exp(prefixes)[..., None, None] * incoming[1]])
    carried = double_sweep_right("clgn,cghpn->clghp", c_half, entry)
    carried = carried * jnp.transpose(jnp.exp(cumulative), (2, 3, 0, 1))[..., None]
    mixed_rows = (inside + carried).reshape(total_len, heads_here * P_SIZE)
    gated_rows = mixed_rows * jax.nn.silu(z_gate.astype(jnp.float32))
    grouped = gated_rows.reshape(total_len, groups_here, per_group * P_SIZE)
    inverse_rms = lax.rsqrt(jnp.mean(grouped * grouped, axis=-1, keepdims=True) + 1e-05)
    scaled = grouped * inverse_rms * gain.reshape(groups_here, per_group * P_SIZE)
    return scaled.reshape(total_len, heads_here * P_SIZE).astype(jnp.bfloat16)


def attention_local(queries, keys, values, pattern):
    total_len = queries.shape[0]
    per_shard = total_len // BLK
    kv_heads = keys.shape[1] // HD
    members = queries.shape[1] // keys.shape[1]
    position = lax.axis_index("ctx")
    stacked = jnp.stack([keys, values])
    window = stacked
    span_now = 1
    while span_now <= REACH:
        arrived = passed_along(window, "ctx", span_now)
        window = jnp.concatenate([arrived, window], axis=1)
        span_now = span_now * 2
    window_blocks = window.reshape(2, -1, BLK, kv_heads, HD)
    first_block = (position - REACH) * per_shard
    local_index = jnp.clip(pattern - first_block, 0, window_blocks.shape[1] - 1)
    key_sel = window_blocks[0][local_index].reshape(per_shard, KSEL * BLK, kv_heads, HD)
    value_sel = window_blocks[1][local_index].reshape(per_shard, KSEL * BLK, kv_heads, HD)
    q_rows = queries.reshape(per_shard, BLK, kv_heads, members, HD)
    scores = jnp.einsum(
        "bqkgd,bmkd->bkgqm", q_rows, key_sel, preferred_element_type=jnp.float32
    ) * HD ** (-0.5)
    key_pos = (pattern[:, :, None] * BLK + jnp.arange(BLK, dtype=jnp.int32)[None, None, :]).reshape(
        per_shard, KSEL * BLK
    )
    query_pos = (position * per_shard + jnp.arange(per_shard, dtype=jnp.int32))[
        :, None
    ] * BLK + jnp.arange(BLK, dtype=jnp.int32)[None, :]
    usable = jnp.repeat(pattern >= 0, BLK, axis=1)
    allowed = usable[:, None, :] & (key_pos[:, None, :] <= query_pos[:, :, None])
    scores = jnp.where(allowed[:, None, None], scores, -jnp.inf)
    row_max = jnp.max(scores, axis=-1, keepdims=True)
    expo = jnp.exp(scores - row_max)
    row_total = jnp.sum(expo, axis=-1)
    rounded = expo.astype(jnp.bfloat16)
    mixed_rows = jnp.einsum(
        "bkgqm,bmkd->bqkgd", rounded, value_sel, preferred_element_type=jnp.float32
    )
    mixed_rows = mixed_rows / jnp.transpose(row_total, (0, 3, 1, 2))[..., None]
    return mixed_rows.reshape(total_len, kv_heads * members * HD).astype(jnp.bfloat16)


def on_device(queries, keys, values, pattern, x_in, z_gate, bmat, cmat, log_decay, gain):
    attn_out = attention_local(queries, keys, values, pattern)
    length = SCAN_BLK
    ssm_out = mamba_mixer(x_in, z_gate, bmat, cmat, log_decay, gain, length)
    return (attn_out, ssm_out)


def solution(mesh):
    placed = (
        P(("groups", "ctx"), "head"),
        P(("groups", "ctx"), "head"),
        P(("groups", "ctx"), "head"),
        P(("groups", "ctx"), None),
        P(("groups", "ctx"), "head"),
        P(("groups", "ctx"), "head"),
        P(("groups", "ctx"), "head"),
        P(("groups", "ctx"), "head"),
        P(("groups", "head"), "ctx"),
        P("head"),
    )
    return jax.shard_map(
        on_device,
        mesh=mesh,
        in_specs=placed,
        out_specs=(P(("groups", "ctx"), "head"), P(("groups", "ctx"), "head")),
        check_vma=False,
    )
```

profile of v0, /device:TPU:0, one launch (start us, length us, event | category | flops | bytes accessed | tf_op | source)
XLA Modules:
  0.0 83.0 jit_solution(15571325007035407345)
XLA Ops:
  7.2 1.0 %reduce_window_sum.11 = f32[1,8,1,128]{3,1,2,0:T(8,128)S(1)} reduce-window(f32[1,8,1,128]{3,1,2,0:T(8,128)} %bitcast.157, f32[]{:T(128)} %constant.58.clone.1), window={size=1x1x1x128 pad=0_0x0_0x0_0x127_0}, to_apply=%region_2.3 | reduce-window | flops 130048 | bytes 8196 | tf_op jit(solution)/shard_map/jit(cumsum)/reduce_window_sum | solution.py:70
  8.4 1.0 %copy.39 = bf16[128,512]{0,1:T(8,128)(2,1)S(1)} copy(bf16[128,512]{1,0:T(8,128)(2,1)} %param.16) | data formatting | bytes 262144 | tf_op args[4]
  9.8 0.9 %fusion.12 = f32[8,64,128]{2,1,0:T(8,128)} fusion(f32[8,64,128]{2,1,0:T(8,128)S(1)} %fusion.52, bf16[128,8,64]{0,2,1:T(8,128)(2,1)S(1)} %bitcast.149, f32[8]{0:T(128)S(1)} %get-tuple-element.136, bf16[128,128]{1,0:T(8,128)(2,1)S(1)} %copy-done), kind=kOutput, calls=%fused_computation.17 | convolution fusion | flops 16908288 | bytes 688160 | tf_op jit(solution)/shard_map/clghp,clgn->cghpn/dot_general | solution.py:51
  10.7 0.9 %pad_maximum_fusion = bf16[2,128,256]{2,1,0:T(8,128)(2,1)S(1)} fusion(bf16[1,128,256]{2,1,0:T(8,128)(2,1)} %bitcast.140, bf16[1,128,256]{2,1,0:T(8,128)(2,1)} %bitcast.143), kind=kLoop, calls=%fused_computation.57 | loop fusion | flops 65536 | bytes 262144 | tf_op jit(solution)/shard_map/stack | solution.py:106
  11.6 4.9 %collective-permute-start = (bf16[2,128,256]{2,1,0:T(8,128)(2,1)S(1)}, bf16[2,128,256]{2,1,0:T(8,128)(2,1)S(1)}, u32[]{:S(2)}, u32[]{:S(2)}) collective-permute-start(bf16[2,128,256]{2,1,0:T(8,128)(2,1)S(1)} %pad_maximum_fusion), channel_id=1, source_target_pairs={{0,2},{2,4},{4,6},{6,8},{8,10},{10,12},{12,14},{1,3},{3,5},{5,7},{... | collective-permute-start | bytes 393224 | tf_op jit(solution)/shard_map/ppermute | solution.py:35
  18.3 0.9 %fusion.60 = f32[128,128]{1,0:T(8,128)S(1)} fusion(bf16[128,128]{1,0:T(8,128)(2,1)} %param.19, bf16[128,128]{1,0:T(8,128)(2,1)S(1)} %copy-done), kind=kOutput, calls=%fused_computation.86 | convolution fusion | flops 4194304 | bytes 131072 | tf_op jit(solution)/shard_map/clgn,cmgn->cglm/dot_general | solution.py:74
  19.3 0.9 %maximum_maximum_fusion.1 = bf16[2,256,256]{2,1,0:T(8,128)(2,1)S(1)} fusion(bf16[1,128,256]{2,1,0:T(8,128)(2,1)} %bitcast.141, bf16[1,128,256]{2,1,0:T(8,128)(2,1)} %bitcast.144, bf16[2,128,256]{2,1,0:T(8,128)(2,1)S(1)} %collective-permute-done), kind=kLoop, calls=%fused_computation.37 | loop fusion | flops 786432 | bytes 524288 | tf_op jit(solution)/shard_map/concatenate | solution.py:111
  20.2 5.3 %collective-permute-start.1 = (bf16[2,256,256]{2,1,0:T(8,128)(2,1)S(1)}, bf16[2,256,256]{2,1,0:T(8,128)(2,1)S(1)}, u32[]{:S(2)}, u32[]{:S(2)}) collective-permute-start(bf16[2,256,256]{2,1,0:T(8,128)(2,1)S(1)} %maximum_maximum_fusion.1), channel_id=1, source_target_pairs={{0,4},{2,6},{4,8},{6,10},{8,12},{10,14},{1,5},{3,7},{5,9},{7,11},{... | collective-permute-start | bytes 786440 | tf_op jit(solution)/shard_map/ppermute | solution.py:35
  25.5 1.1 %reshape.353 = bf16[128,2,4,128]{3,2,1,0:T(4,128)(2,1)S(1)} reshape(bf16[128,1024]{1,0:T(8,128)(2,1)} %param.12) | data formatting | bytes 524288 | tf_op jit(solution)/shard_map/reshape.25
  26.7 24.1 %all-gather = f32[8,8,1,1]{1,3,2,0:T(1,128)S(1)} all-gather(f32[1,8,1,1]{1,3,2,0:T(1,128)S(1)} %copy.40), channel_id=2, replica_groups=mesh['groups'=2,'ctx'=8,'head'=2] {'ctx'}, dimensions={0}, use_global_device_ids=true | all-gather | bytes 288 | tf_op jit(solution)/shard_map/all_gather | solution.py:17
  51.4 1.6 %gather_fusion.1 = bf16[8,128,2,128]{3,2,1,0:T(2,128)(2,1)S(1)} fusion(bf16[4,128,2,128]{3,2,1,0:T(2,128)(2,1)S(1)} %squeeze.18, s32[1024]{0:T(1024)S(1)} %pad_clamp_fusion), kind=kCustom, calls=%fused_computation.1 | custom fusion | bytes 1048608 | tf_op jit(solution)/shard_map/gather | solution.py:116
  53.2 1.6 %gather_fusion = bf16[8,128,2,128]{3,2,1,0:T(2,128)(2,1)S(1)} fusion(bf16[4,128,2,128]{3,2,1,0:T(2,128)(2,1)S(1)} %squeeze.17, s32[1024]{0:T(1024)S(1)} %pad_clamp_fusion), kind=kCustom, calls=%fused_computation | custom fusion | bytes 1048608 | tf_op jit(solution)/shard_map/gather | solution.py:117
  55.5 0.9 %fusion.1 = f32[2,4,128]{2,1,0:T(4,128)S(1)} fusion(f32[2,1024,128,4]{2,1,3,0:T(8,128)S(1)} %get-tuple-element.158, f32[2,4,128]{2,1,0:T(4,128)S(1)} %get-tuple-element.157, pred[128,1024]{0,1:T(8,128)(4,1)S(1)} %compare_and_fusion), kind=kLoop, calls=%fused_computation.7 | loop fusion | flops 4193280 | bytes 4333568 | tf_op jit(solution)/shard_map/reduce_sum | solution.py:133
  56.4 1.1 %fusion.19 = bf16[1,128,2,4,128]{1,4,3,2,0:T(8,128)(2,1)S(1)} fusion(f32[2,1024,128,4]{2,1,3,0:T(8,128)S(1)} %get-tuple-element.158, f32[2,4,128]{2,1,0:T(4,128)S(1)} %get-tuple-element.157, pred[128,1024]{0,1:T(8,128)(4,1)S(1)} %compare_and_fusion, bf16[1024,2,128,1]{2,1,0,3:T(2,128)(2,1)S(1)} %bitcast.150, f32[128,2,4]{0,2,1:T(4,128)S(1)} %bitcast.158), kind=kOutput, calls=%fused_computation.23 | convolution fusion | flops 272891904 | bytes 5120000 | tf_op jit(solution)/shard_map/bkgqm,bmkd->bqkgd/dot_general | solution.py:135
  58.4 7.2 %all-gather.4.cloned.1.call-done = f32[64,64,128]{2,1,0:T(8,128)} async-done(((f32[8,64,128]{2,1,0:T(8,128)}), f32[64,64,128]{2,1,0:T(8,128)}) %all-gather.4.cloned.1.call-update) | async-done | bytes 2097168 | tf_op jit(solution)/shard_map/all_gather | solution.py:17
  65.6 8.7 %while.14 = (s32[]{:T(128)}, f32[1,8,64,128]{3,2,1,0:T(8,128)S(1)}, s32[]{:T(128)}, f32[8,1,8]{2,1,0:T(1,128)S(1)}, f32[8,1,8,64,128]{4,3,2,1,0:T(8,128)}, /*index=5*/s32[]{:T(128)}, s32[]{:T(128)}) while((s32[]{:T(128)}, f32[1,8,64,128]{3,2,1,0:T(8,128)S(1)}, s32[]{:T(128)}, f32[8,1,8]{2,1,0:T(1,128)S(1)}, ...), condition=%wide.region_4.5_spmd.clone, body=%wide.region_3.4_spmd.clone.sunk | while | flops 262148 | bytes 786641 | solution.py:29
  65.6 1.1 %fusion.69 = f32[1,8,64,128]{3,2,1,0:T(8,128)S(1)} fusion(f32[8,1,8,64,128]{4,3,2,1,0:T(8,128)} %get-tuple-element.208, s32[]{:T(128)S(6)} %copy.60, f32[1,8,64,128]{3,2,1,0:T(8,128)S(1)} %get-tuple-element.198, f32[8]{0:T(128)S(1)} %exponential_bitcast_fusion.4, pred[]{:T(512)S(6)} %compare.3, pred[]{:T(512)S(6)} %lt.30), kind=kLoop, calls=%fused_computation.3.clone.1 | loop fusion | flops 262144 | bytes 786470 | tf_op jit(solution)/shard_map/while/body/eval_jaxpr/jit(_where)/select_n | solution.py:27
  66.7 1.1 %fusion.69 = f32[1,8,64,128]{3,2,1,0:T(8,128)S(1)} fusion(f32[8,1,8,64,128]{4,3,2,1,0:T(8,128)} %get-tuple-element.208, s32[]{:T(128)S(6)} %copy.60, f32[1,8,64,128]{3,2,1,0:T(8,128)S(1)} %get-tuple-element.198, f32[8]{0:T(128)S(1)} %exponential_bitcast_fusion.4, pred[]{:T(512)S(6)} %compare.3, pred[]{:T(512)S(6)} %lt.30), kind=kLoop, calls=%fused_computation.3.clone.1 | loop fusion | flops 262144 | bytes 786470 | tf_op jit(solution)/shard_map/while/body/eval_jaxpr/jit(_where)/select_n | solution.py:27
  67.8 1.1 %fusion.69 = f32[1,8,64,128]{3,2,1,0:T(8,128)S(1)} fusion(f32[8,1,8,64,128]{4,3,2,1,0:T(8,128)} %get-tuple-element.208, s32[]{:T(128)S(6)} %copy.60, f32[1,8,64,128]{3,2,1,0:T(8,128)S(1)} %get-tuple-element.198, f32[8]{0:T(128)S(1)} %exponential_bitcast_fusion.4, pred[]{:T(512)S(6)} %compare.3, pred[]{:T(512)S(6)} %lt.30), kind=kLoop, calls=%fused_computation.3.clone.1 | loop fusion | flops 262144 | bytes 786470 | tf_op jit(solution)/shard_map/while/body/eval_jaxpr/jit(_where)/select_n | solution.py:27
  68.9 1.1 %fusion.69 = f32[1,8,64,128]{3,2,1,0:T(8,128)S(1)} fusion(f32[8,1,8,64,128]{4,3,2,1,0:T(8,128)} %get-tuple-element.208, s32[]{:T(128)S(6)} %copy.60, f32[1,8,64,128]{3,2,1,0:T(8,128)S(1)} %get-tuple-element.198, f32[8]{0:T(128)S(1)} %exponential_bitcast_fusion.4, pred[]{:T(512)S(6)} %compare.3, pred[]{:T(512)S(6)} %lt.30), kind=kLoop, calls=%fused_computation.3.clone.1 | loop fusion | flops 262144 | bytes 786470 | tf_op jit(solution)/shard_map/while/body/eval_jaxpr/jit(_where)/select_n | solution.py:27
  70.0 1.1 %fusion.69 = f32[1,8,64,128]{3,2,1,0:T(8,128)S(1)} fusion(f32[8,1,8,64,128]{4,3,2,1,0:T(8,128)} %get-tuple-element.208, s32[]{:T(128)S(6)} %copy.60, f32[1,8,64,128]{3,2,1,0:T(8,128)S(1)} %get-tuple-element.198, f32[8]{0:T(128)S(1)} %exponential_bitcast_fusion.4, pred[]{:T(512)S(6)} %compare.3, pred[]{:T(512)S(6)} %lt.30), kind=kLoop, calls=%fused_computation.3.clone.1 | loop fusion | flops 262144 | bytes 786470 | tf_op jit(solution)/shard_map/while/body/eval_jaxpr/jit(_where)/select_n | solution.py:27
  71.1 1.1 %fusion.69 = f32[1,8,64,128]{3,2,1,0:T(8,128)S(1)} fusion(f32[8,1,8,64,128]{4,3,2,1,0:T(8,128)} %get-tuple-element.208, s32[]{:T(128)S(6)} %copy.60, f32[1,8,64,128]{3,2,1,0:T(8,128)S(1)} %get-tuple-element.198, f32[8]{0:T(128)S(1)} %exponential_bitcast_fusion.4, pred[]{:T(512)S(6)} %compare.3, pred[]{:T(512)S(6)} %lt.30), kind=kLoop, calls=%fused_computation.3.clone.1 | loop fusion | flops 262144 | bytes 786470 | tf_op jit(solution)/shard_map/while/body/eval_jaxpr/jit(_where)/select_n | solution.py:27
  72.2 1.1 %fusion.69 = f32[1,8,64,128]{3,2,1,0:T(8,128)S(1)} fusion(f32[8,1,8,64,128]{4,3,2,1,0:T(8,128)} %get-tuple-element.208, s32[]{:T(128)S(6)} %copy.60, f32[1,8,64,128]{3,2,1,0:T(8,128)S(1)} %get-tuple-element.198, f32[8]{0:T(128)S(1)} %exponential_bitcast_fusion.4, pred[]{:T(512)S(6)} %compare.3, pred[]{:T(512)S(6)} %lt.30), kind=kLoop, calls=%fused_computation.3.clone.1 | loop fusion | flops 262144 | bytes 786470 | tf_op jit(solution)/shard_map/while/body/eval_jaxpr/jit(_where)/select_n | solution.py:27
  73.3 1.1 %fusion.69 = f32[1,8,64,128]{3,2,1,0:T(8,128)S(1)} fusion(f32[8,1,8,64,128]{4,3,2,1,0:T(8,128)} %get-tuple-element.208, s32[]{:T(128)S(6)} %copy.60, f32[1,8,64,128]{3,2,1,0:T(8,128)S(1)} %get-tuple-element.198, f32[8]{0:T(128)S(1)} %exponential_bitcast_fusion.4, pred[]{:T(512)S(6)} %compare.3, pred[]{:T(512)S(6)} %lt.30), kind=kLoop, calls=%fused_computation.3.clone.1 | loop fusion | flops 262144 | bytes 786470 | tf_op jit(solution)/shard_map/while/body/eval_jaxpr/jit(_where)/select_n | solution.py:27
  (54 shorter events, 6.7 us)
Async XLA Ops:
  7.2 2.4 %copy-start = (bf16[128,128]{1,0:T(8,128)(2,1)S(1)}, bf16[128,128]{1,0:T(8,128)(2,1)}, u32[]{:S(2)}) copy-start(bf16[128,128]{1,0:T(8,128)(2,1)} %param.18) | copy-start | bytes 98308
  7.2 44.0 %copy-start.1 = (bf16[128,256]{1,0:T(8,128)(2,1)S(1)}, bf16[128,256]{1,0:T(8,128)(2,1)}, u32[]{:S(2)}) copy-start(bf16[128,256]{1,0:T(8,128)(2,1)} %param.14) | copy-start | bytes 196612
  7.2 44.0 %copy-start.2 = (bf16[128,256]{1,0:T(8,128)(2,1)S(1)}, bf16[128,256]{1,0:T(8,128)(2,1)}, u32[]{:S(2)}) copy-start(bf16[128,256]{1,0:T(8,128)(2,1)} %param.13) | copy-start | bytes 196612
  7.2 58.4 %all-gather.4.cloned.1.call-start = ((), (), s32[]{:S(2)}) async-start(), calls=%async_computation | async-start | bytes 2359296 | tf_op jit(solution)/shard_map/all_gather | solution.py:17
  11.6 7.7 %collective-permute-start = (bf16[2,128,256]{2,1,0:T(8,128)(2,1)S(1)}, bf16[2,128,256]{2,1,0:T(8,128)(2,1)S(1)}, u32[]{:S(2)}, u32[]{:S(2)}) collective-permute-start(bf16[2,128,256]{2,1,0:T(8,128)(2,1)S(1)} %pad_maximum_fusion), channel_id=1, source_target_pairs={{0,2},{2,4},{4,6},{6,8},{8,10},{10,12},{12,14},{1,3},{3,5},{5,7},{... | collective-permute-start | bytes 393224 | tf_op jit(solution)/shard_map/ppermute | solution.py:35
  20.2 31.0 %collective-permute-start.1 = (bf16[2,256,256]{2,1,0:T(8,128)(2,1)S(1)}, bf16[2,256,256]{2,1,0:T(8,128)(2,1)S(1)}, u32[]{:S(2)}, u32[]{:S(2)}) collective-permute-start(bf16[2,256,256]{2,1,0:T(8,128)(2,1)S(1)} %maximum_maximum_fusion.1), channel_id=1, source_target_pairs={{0,4},{2,6},{4,8},{6,10},{8,12},{10,14},{1,5},{3,7},{5,9},{7,11},{... | collective-permute-start | bytes 786440 | tf_op jit(solution)/shard_map/ppermute | solution.py:35
  57.5 16.8 %copy-start.4 = (bf16[128,128]{1,0:T(8,128)(2,1)S(1)}, bf16[128,128]{1,0:T(8,128)(2,1)}, u32[]{:S(2)}) copy-start(bf16[128,128]{1,0:T(8,128)(2,1)} %param.19) | copy-start | bytes 98308
  57.5 17.7 %copy-start.3 = (bf16[128,512]{1,0:T(8,128)(2,1)S(1)}, bf16[128,512]{1,0:T(8,128)(2,1)}, u32[]{:S(2)}) copy-start(bf16[128,512]{1,0:T(8,128)(2,1)} %param.17) | copy-start | bytes 393220
  57.5 17.9 %copy-start.5 = (f32[512]{0:T(512)S(1)}, f32[512]{0:T(512)}, u32[]{:S(2)}) copy-start(f32[512]{0:T(512)} %param.21) | copy-start | bytes 6148
Sparse Core Ops, SparseCore 0:
  10.8 54.7 all-gather.3
where the time goes:
time: 83.7 us; the launch traced here: 83 us
  blocking collectives  24.1 us (29%)
  other arithmetic  15.1 us (18%)
  between operations  14.3 us (17%)
  starting transfers between devices  10.3 us (12%)
  waiting for transfers between devices  7.23 us (9%)
  local copies, waits for them, and re-layouts  6.94 us (8%)
  matrix products  4.89 us (6%)
    all_gather x1, blocking collectives, entering(): everything = jax.tree.map(lambda part: lax.all_gather(part, axis), shard)  24.1 us
    ppermute x2, starting transfers between devices, passed_along(): lax.ppermute(value, axis, [(source, source + steps) for source in range(i...  10.2 us
    select_n x8, other arithmetic, step(): return jax.tree.map(lambda a, b: jnp.where(reached, a, b), new, before)  8.42 us
    all_gather x1, waiting for transfers between devices, entering(): everything = jax.tree.map(lambda part: lax.all_gather(part, axis), shard)  7.21 us
    unnamed x14, local copies, waits for them, and re-layouts  1.92 us
    gather x2, local copies, waits for them, and re-layouts, attention_local(): window_blocks[0][local_index].reshape(per_shard, KSEL * BLK, kv_heads, HD)  1.7 us
  transfers between devices with their start and end apart: 3, of which 1 were waited for; matrix products, arithmetic and copies ran while one was open for 16% of the time, Pallas kernels for 0%

commit v1 on v0

v1 whole, which is shorter than its diff:
```python
import jax
import jax.numpy as jnp
from jax import lax
from jax.experimental import pallas as pl
from jax.experimental.pallas import tpu as pltpu
from jax.sharding import PartitionSpec as P

BLK = 128
HD = 128
P_SIZE = 64
N = 128
EPS = 1e-05
F32 = jnp.float32
BF16 = jnp.bfloat16
HIGHEST = lax.Precision.HIGHEST
EXTRA = 16


def whole(count):
    return [pl.BlockSpec(memory_space=pltpu.VMEM)] * count


def dot(a, b, dims=((1,), (0,)), precision=None):
    return lax.dot_general(a, b, (dims, ((), ())), precision=precision, preferred_element_type=F32)


def iota(shape, axis):
    return lax.broadcasted_iota(jnp.int32, shape, axis)


def per_channel(per_head, heads):
    width = heads * P_SIZE
    spread = jnp.where(iota((heads, width), 1) // P_SIZE == iota((heads, width), 0), 1.0, 0.0).astype(BF16)
    upper = per_head.astype(BF16)
    lower = (per_head - upper.astype(F32)).astype(BF16)
    return dot(upper, spread) + dot(lower, spread)


def decay_row(ref):
    tail = ref[N : N + EXTRA, :].astype(F32)
    return tail[0:1] + tail[EXTRA // 2 : EXTRA // 2 + 1]


def with_decay(ref, decay):
    upper = decay.astype(BF16).astype(F32)
    ref[N : N + EXTRA, :] = jnp.concatenate([upper, decay - upper], axis=0).astype(BF16)


def summary_kernel(x_ref, b_ref, rate_ref, k_ref, v_ref, state_ref, kv_ref):
    rates = rate_ref[...]
    heads, length = rates.shape
    later = jnp.where(iota((length, length), 1) > iota((length, length), 0), 1.0, 0.0)
    to_end = dot(later, rates, ((1,), (1,)), HIGHEST)
    weighted = x_ref[...].astype(F32) * per_channel(jnp.exp(to_end), heads)
    state = dot(b_ref[...], weighted.astype(BF16), ((0,), (0,)))
    state_ref[0:N, :] = state.astype(BF16)
    total = dot(jnp.ones((8, length), F32), rates, ((1,), (1,)), HIGHEST)
    with_decay(state_ref, per_channel(jnp.exp(total), heads))
    kv_ref[0:BLK, :] = k_ref[...]
    kv_ref[BLK : 2 * BLK, :] = v_ref[...]


def combine_kernel(bit, mine_ref, other_ref, out_ref):
    mine, other = decay_row(mine_ref), decay_row(other_ref)
    is_later = (lax.axis_index("ctx") & bit) != 0
    keep = jnp.where(is_later, jnp.ones_like(other), other)
    take = jnp.where(is_later, mine, jnp.ones_like(mine))
    state = keep * mine_ref[0:N, :].astype(F32) + take * other_ref[0:N, :].astype(F32)
    out_ref[0:N, :] = state.astype(BF16)
    with_decay(out_ref, jnp.broadcast_to(mine * other, (8, mine.shape[1])))


def inside_kernel(bits, x_ref, b_ref, c_ref, rate_ref, z_ref, *refs):
    received, (base_ref, factor_ref) = refs[:-2], refs[-2:]
    rates = rate_ref[...]
    heads, length = rates.shape
    row, col = iota((length, length), 0), iota((length, length), 1)
    upto = jnp.where(col <= row, 1.0, 0.0)
    cum_cols = dot(upto, rates, ((1,), (1,)), HIGHEST)
    cum_rows = dot(rates, upto, ((1,), (1,)), HIGHEST)
    c_half = c_ref[...]
    affinity = dot(c_half, b_ref[...], ((1,), (1,)))
    parts = []
    for head in range(heads):
        spread = cum_cols[:, head : head + 1] - cum_rows[head : head + 1, :]
        mixing = affinity * jnp.exp(jnp.where(col <= row, spread, -jnp.inf))
        parts.append(dot(mixing.astype(BF16), x_ref[:, head * P_SIZE : (head + 1) * P_SIZE]))
    inside = jnp.concatenate(parts, axis=1)
    position = lax.axis_index("ctx")
    since = jnp.ones((1, heads * P_SIZE), F32)
    carried = jnp.zeros((length, heads * P_SIZE), F32)
    for bit, ref in zip(bits, received):
        is_later = (position & bit) != 0
        share = jnp.where(is_later, since, jnp.zeros_like(since))
        carried = carried + dot(c_half, ref[0:N, :]) * share
        since = jnp.where(is_later, since * decay_row(ref), since)
    reach = per_channel(jnp.exp(cum_cols), heads)
    z = z_ref[...].astype(F32)
    gate = z / (1.0 + jnp.exp(-z))
    base_ref[...] = (inside + carried * reach) * gate
    last = jnp.where((position & bits[-1]) != 0, since, jnp.zeros_like(since))
    factor_ref[...] = reach * last * gate


def finish_kernel(c_ref, state_ref, base_ref, factor_ref, gain_ref, out_ref):
    gated = base_ref[...] + factor_ref[...] * dot(c_ref[...], state_ref[0:N, :])
    inverse = lax.rsqrt(jnp.mean(gated * gated, axis=-1, keepdims=True) + EPS)
    out_ref[...] = (gated * inverse * gain_ref[...]).astype(BF16)


def attention_kernel(pattern_ref, q_ref, own_ref, two_ref, cross_ref, third_ref, pair_ref, out_ref):
    position = lax.axis_index("ctx")
    even = (position & 1) == 0

    def listed(block):
        hit = pattern_ref[0, 1] == block
        for entry in range(2, pattern_ref.shape[1]):
            hit = hit | (pattern_ref[0, entry] == block)
        return hit & (block >= 0)

    blocks = [position - 2, (position ^ 1) - 2, jnp.where(even, position - 3, position - 1)]
    last = jnp.where(even, third_ref[...], pair_ref[...])
    sources = [own_ref[...], two_ref[...], cross_ref[...], last]
    members = q_ref.shape[1] // own_ref.shape[1]
    rows = members * BLK
    causal = iota((rows, BLK), 1) <= (iota((rows, BLK), 0) & (BLK - 1))
    for kv_head in range(own_ref.shape[1] // HD):
        cols = slice(kv_head * HD, (kv_head + 1) * HD)
        at = [(kv_head * members + member) * HD for member in range(members)]
        q = jnp.concatenate([q_ref[:, a : a + HD] for a in at], axis=0)
        scores = []
        for order, source in enumerate(sources):
            part = dot(q, source[0:BLK, cols], ((1,), (1,))) * HD ** (-0.5)
            keep = causal if order == 0 else listed(blocks[order - 1])
            scores.append(jnp.where(keep, part, -jnp.inf))
        scores = jnp.concatenate(scores, axis=1)
        expo = jnp.exp(scores - jnp.max(scores, axis=-1, keepdims=True))
        total = jnp.sum(expo, axis=-1, keepdims=True)
        values = jnp.concatenate([source[BLK : 2 * BLK, cols] for source in sources], axis=0)
        mixed = dot(expo.astype(BF16), values) / total
        for member, a in enumerate(at):
            out_ref[:, a : a + HD] = mixed[member * BLK : (member + 1) * BLK].astype(BF16)


def call(kernel, out, *args, flops=1000000, moved=1000000, specs=None):
    return pl.pallas_call(
        kernel,
        out_shape=out,
        in_specs=specs or whole(len(args)),
        out_specs=jax.tree.map(lambda _: pl.BlockSpec(memory_space=pltpu.VMEM), out),
        cost_estimate=pl.CostEstimate(flops=flops, bytes_accessed=moved, transcendentals=0),
    )(*args)


def on_device(queries, keys, values, pattern, x_in, z_gate, bmat, cmat, log_decay, gain):
    count = lax.axis_size("ctx")
    tokens, width = x_in.shape
    bits = [1 << power for power in range((count - 1).bit_length())]
    shape = jax.ShapeDtypeStruct
    state_shape = shape((N + EXTRA, width), BF16)

    def swapped(value, bit):
        return lax.ppermute(value, "ctx", [(k, k ^ bit) for k in range(count)])

    state, kv = call(
        summary_kernel,
        (state_shape, shape((2 * BLK, keys.shape[1]), BF16)),
        x_in, bmat, log_decay, keys, values,
    )
    two = lax.ppermute(kv, "ctx", [(k, (k + 2) % count) for k in range(count)])
    pair = swapped(kv, 1)
    cross = swapped(two, 1)
    ends = [(0, 0), (count - 1, count - 1)]
    inner = [(k, k + 1 if k % 2 else k - 1) for k in range(1, count - 1)]
    third = lax.ppermute(two, "ctx", ends + inner)

    received = []
    for order, bit in enumerate(bits):
        other = swapped(state, bit)
        received.append(other)
        if order + 1 < len(bits):
            state = call(lambda *refs, bit=bit: combine_kernel(bit, *refs), state_shape, state, other)

    wide = shape((tokens, width), F32)
    base, factor = call(
        lambda *refs: inside_kernel(bits, *refs), (wide, wide),
        x_in, bmat, cmat, log_decay, z_gate, *received[:-1],
    )
    attn_out = call(
        attention_kernel, shape(queries.shape, BF16),
        pattern, queries, kv, two, cross, third, pair,
        specs=[pl.BlockSpec(memory_space=pltpu.SMEM)] + whole(6),
    )
    ssm_out = call(
        finish_kernel, shape((tokens, width), BF16),
        cmat, received[-1], base, factor, gain.reshape(1, width),
    )
    return (attn_out, ssm_out)


def solution(mesh):
    rows = P(("groups", "ctx"), "head")
    placed = (rows, rows, rows, P(("groups", "ctx"), None), rows, rows, rows, rows, P(("groups", "head"), "ctx"), P("head"))
    return jax.shard_map(on_device, mesh=mesh, in_specs=placed, out_specs=(rows, rows), check_vma=False)
```

time: 83.7 us -> 41.9 us (0.50)
  the two profiles are of different devices: /device:TPU:0 before, /device:TPU:8 now
where the time goes in v1:
time: 41.9 us; the launch traced here: 41.6 us
  Pallas kernels  13.8 us (33%)
  starting transfers between devices  12.5 us (30%)
  waiting for transfers between devices  12 us (29%)
  local copies, waits for them, and re-layouts  2.65 us (6%)
  between operations  0.67 us (2%)
    pallas_call x6, Pallas kernels, call(): pl.pallas_call(kernel, out_shape=out, in_specs=specs or whole(len(args)),...  13.8 us
    ppermute x5, waiting for transfers between devices, swapped(): return lax.ppermute(value, 'ctx', [(k, k ^ bit) for k in range(count)])  9.88 us
    ppermute x5, starting transfers between devices, swapped(): return lax.ppermute(value, 'ctx', [(k, k ^ bit) for k in range(count)])  6.31 us
    ppermute x1, starting transfers between devices, on_device(): third = lax.ppermute(two, 'ctx', ends + inner)  3.27 us
    ppermute x1, starting transfers between devices, on_device(): two = lax.ppermute(kv, 'ctx', [(k, (k + 2) % count) for k in range(count)])  2.96 us
    unnamed x16, local copies, waits for them, and re-layouts  2.65 us
    ppermute x1, waiting for transfers between devices, on_device(): third = lax.ppermute(two, 'ctx', ends + inner)  2.08 us
  transfers between devices with their start and end apart: 7, of which 5 were waited for; matrix products, arithmetic and copies ran while one was open for 0% of the time, Pallas kernels for 19%

profile of v1, /device:TPU:8, one launch (start us, length us, event | category | flops | bytes accessed | tf_op | source)
XLA Modules:
  0.0 41.6 jit_solution(9869678065216153090)
XLA Ops:
  0.6 2.3 %shard_map.113 = (bf16[144,512]{1,0:T(8,128)(2,1)}, bf16[256,256]{1,0:T(8,128)(2,1)}) custom-call(bf16[128,512]{1,0:T(8,128)(2,1)} %refs_0_.1, bf16[128,128]{1,0:T(8,128)(2,1)} %refs_1_.1, f32[8,128]{1,0:T(8,128)} %refs_3_.1, bf16[128,256]{1,0:T(8,128)(2,1)} %k_ref.1, bf16[128,256]{1,0:T(8,128)(2,1)} %v_ref.1), custom_call_target="tpu_custom_call" | custom-call | flops 1000000 | bytes 1000000 | tf_op jit(solution)/shard_map/pallas_call | solution.py:146
  2.9 1.5 %collective-permute-start.4 = (bf16[144,512]{1,0:T(8,128)(2,1)}, bf16[144,512]{1,0:T(8,128)(2,1)S(1)}, u32[]{:S(2)}, u32[]{:S(2)}) collective-permute-start(bf16[144,512]{1,0:T(8,128)(2,1)} %get-tuple-element.7.refs_0_), channel_id=1, source_target_pairs={{0,2},{2,0},{4,6},{6,4},{8,10},{10,8},{12,14},{14,12},{1,3},{3,1},... | collective-permute-start | bytes 442376 | tf_op jit(solution)/shard_map/ppermute | solution.py:163
  4.4 4.3 %collective-permute-done.4.refs_1_.refs_5_ = bf16[144,512]{1,0:T(8,128)(2,1)S(1)} collective-permute-done((bf16[144,512]{1,0:T(8,128)(2,1)}, bf16[144,512]{1,0:T(8,128)(2,1)S(1)}, u32[]{:S(2)}, u32[]{:S(2)}) %collective-permute-start.4) | collective-permute-done | bytes 147488 | tf_op jit(solution)/shard_map/ppermute | solution.py:163
  8.7 0.7 %copy-done = bf16[144,512]{1,0:T(8,128)(2,1)} copy-done((bf16[144,512]{1,0:T(8,128)(2,1)}, bf16[144,512]{1,0:T(8,128)(2,1)S(1)}, u32[]{:S(2)}) %copy-start) | copy-done | bytes 147480
  9.4 1.7 %shard_map.115.refs_0_ = bf16[144,512]{1,0:T(8,128)(2,1)} custom-call(bf16[144,512]{1,0:T(8,128)(2,1)} %get-tuple-element.7.refs_0_, bf16[144,512]{1,0:T(8,128)(2,1)} %copy-done), custom_call_target="tpu_custom_call" | custom-call | flops 1000000 | bytes 1000000 | tf_op jit(solution)/shard_map/pallas_call | solution.py:146
  11.1 0.2 collective-permute-start.5
  11.3 3.0 %collective-permute-start = (bf16[256,256]{1,0:T(8,128)(2,1)S(1)}, bf16[256,256]{1,0:T(8,128)(2,1)S(1)}, u32[]{:S(2)}, u32[]{:S(2)}) collective-permute-start(bf16[256,256]{1,0:T(8,128)(2,1)S(1)} %copy-done.3), channel_id=1, source_target_pairs={{0,4},{2,6},{4,8},{6,10},{8,12},{10,14},{12,0},{14,2},{1,5},{3,7},... | collective-permute-start | bytes 393224 | tf_op jit(solution)/shard_map/ppermute | solution.py:170
  14.2 3.2 %collective-permute-done.5.refs_1_.refs_6_ = bf16[144,512]{1,0:T(8,128)(2,1)S(1)} collective-permute-done((bf16[144,512]{1,0:T(8,128)(2,1)}, bf16[144,512]{1,0:T(8,128)(2,1)S(1)}, u32[]{:S(2)}, u32[]{:S(2)}) %collective-permute-start.5) | collective-permute-done | bytes 147488 | tf_op jit(solution)/shard_map/ppermute | solution.py:163
  17.4 0.7 %copy-done.1 = bf16[144,512]{1,0:T(8,128)(2,1)} copy-done((bf16[144,512]{1,0:T(8,128)(2,1)}, bf16[144,512]{1,0:T(8,128)(2,1)S(1)}, u32[]{:S(2)}) %copy-start.1) | copy-done | bytes 147480
  18.1 1.7 %shard_map.116 = bf16[144,512]{1,0:T(8,128)(2,1)} custom-call(bf16[144,512]{1,0:T(8,128)(2,1)} %shard_map.115.refs_0_, bf16[144,512]{1,0:T(8,128)(2,1)} %copy-done.1), custom_call_target="tpu_custom_call" | custom-call | flops 1000000 | bytes 1000000 | tf_op jit(solution)/shard_map/pallas_call | solution.py:146
  19.8 2.6 %collective-permute-start.6 = (bf16[144,512]{1,0:T(8,128)(2,1)}, bf16[144,512]{1,0:T(8,128)(2,1)S(1)}, u32[]{:S(2)}, u32[]{:S(2)}) collective-permute-start(bf16[144,512]{1,0:T(8,128)(2,1)} %shard_map.116), channel_id=1, source_target_pairs={{0,8},{2,10},{4,12},{6,14},{8,0},{10,2},{12,4},{14,6},{1,9},{3,11}... | collective-permute-start | bytes 442376 | tf_op jit(solution)/shard_map/ppermute | solution.py:163
  22.4 1.5 %collective-permute-start.3 = (bf16[256,256]{1,0:T(8,128)(2,1)S(1)}, bf16[256,256]{1,0:T(8,128)(2,1)S(1)}, u32[]{:S(2)}, u32[]{:S(2)}) collective-permute-start(bf16[256,256]{1,0:T(8,128)(2,1)S(1)} %copy-done.3), channel_id=1, source_target_pairs={{0,2},{2,0},{4,6},{6,4},{8,10},{10,8},{12,14},{14,12},{1,3},{3,1},... | collective-permute-start | bytes 393224 | tf_op jit(solution)/shard_map/ppermute | solution.py:163
  23.9 0.0 collective-permute-done.two_ref
  23.9 0.5 %collective-permute-start.1 = (bf16[256,256]{1,0:T(8,128)(2,1)S(1)}, bf16[256,256]{1,0:T(8,128)(2,1)S(1)}, u32[]{:S(2)}, u32[]{:S(2)}) collective-permute-start(bf16[256,256]{1,0:T(8,128)(2,1)S(1)} %collective-permute-done.two_ref), channel_id=1, source_target_pairs={{0,2},{2,0},{4,6},{6,4},{8,10},{10,8},{12,14},{14,12},{1,3},{3,1},... | collective-permute-start | bytes 393224 | tf_op jit(solution)/shard_map/ppermute | solution.py:163
  24.4 3.3 %collective-permute-start.2 = (bf16[256,256]{1,0:T(8,128)(2,1)S(1)}, bf16[256,256]{1,0:T(8,128)(2,1)S(1)}, u32[]{:S(2)}, u32[]{:S(2)}) collective-permute-start(bf16[256,256]{1,0:T(8,128)(2,1)S(1)} %collective-permute-done.two_ref), channel_id=1, source_target_pairs={{0,0},{14,14},{2,4},{4,2},{6,8},{8,6},{10,12},{12,10},{1,1},{15,15... | collective-permute-start | bytes 393224 | tf_op jit(solution)/shard_map/ppermute | solution.py:175
  27.7 1.0 %collective-permute-done.3.pair_ref = bf16[256,256]{1,0:T(8,128)(2,1)S(1)} collective-permute-done((bf16[256,256]{1,0:T(8,128)(2,1)S(1)}, bf16[256,256]{1,0:T(8,128)(2,1)S(1)}, u32[]{:S(2)}, u32[]{:S(2)}) %collective-permute-start.3) | collective-permute-done | bytes 131104 | tf_op jit(solution)/shard_map/ppermute | solution.py:163
  28.7 1.4 %collective-permute-done.1.cross_ref = bf16[256,256]{1,0:T(8,128)(2,1)S(1)} collective-permute-done((bf16[256,256]{1,0:T(8,128)(2,1)S(1)}, bf16[256,256]{1,0:T(8,128)(2,1)S(1)}, u32[]{:S(2)}, u32[]{:S(2)}) %collective-permute-start.1) | collective-permute-done | bytes 131104 | tf_op jit(solution)/shard_map/ppermute | solution.py:163
  30.1 2.1 %collective-permute-done.2.third_ref = bf16[256,256]{1,0:T(8,128)(2,1)S(1)} collective-permute-done((bf16[256,256]{1,0:T(8,128)(2,1)S(1)}, bf16[256,256]{1,0:T(8,128)(2,1)S(1)}, u32[]{:S(2)}, u32[]{:S(2)}) %collective-permute-start.2) | collective-permute-done | bytes 131104 | tf_op jit(solution)/shard_map/ppermute | solution.py:175
  32.2 0.6 %copy-done.7 = bf16[256,256]{1,0:T(8,128)(2,1)} copy-done((bf16[256,256]{1,0:T(8,128)(2,1)}, bf16[256,256]{1,0:T(8,128)(2,1)S(1)}, u32[]{:S(2)}) %copy-start.7) | copy-done | bytes 131096
  32.8 3.3 %shard_map.114 = bf16[128,1024]{1,0:T(8,128)(2,1)} custom-call(s32[1,8]{1,0:T(1,128)} %pattern_ref.1, bf16[128,1024]{1,0:T(8,128)(2,1)} %q_ref.1, bf16[256,256]{1,0:T(8,128)(2,1)} %get-tuple-element.6.own_ref, bf16[256,256]{1,0:T(8,128)(2,1)} %copy-done.4, bf16[256,256]{1,0:T(8,128)(2,1)} %copy-done.6, bf16[256,256]{1,0:T(8,128)(2,1)} %copy-done.7, ...), custom_call_target="tpu_custom_call" | custom-call | flops 1000000 | bytes 1000000 | tf_op jit(solution)/shard_map/pallas_call | solution.py:146
  36.1 2.8 %shard_map.117 = (f32[128,512]{1,0:T(8,128)}, f32[128,512]{1,0:T(8,128)}) custom-call(bf16[128,512]{1,0:T(8,128)(2,1)} %refs_0_.1, bf16[128,128]{1,0:T(8,128)(2,1)} %refs_1_.1, bf16[128,128]{1,0:T(8,128)(2,1)} %c_ref.1, f32[8,128]{1,0:T(8,128)} %refs_3_.1, bf16[128,512]{1,0:T(8,128)(2,1)} %refs_4_.1, bf16[144,512]{1,0:T(8,128)(2,1)} %copy-done, ...), custom_call_target="tpu_custom_call" | custom-call | flops 1000000 | bytes 1000000 | tf_op jit(solution)/shard_map/pallas_call | solution.py:146
  38.9 0.0 collective-permute-done.6.state_ref
  38.9 0.7 %copy-done.2 = bf16[144,512]{1,0:T(8,128)(2,1)} copy-done((bf16[144,512]{1,0:T(8,128)(2,1)}, bf16[144,512]{1,0:T(8,128)(2,1)S(1)}, u32[]{:S(2)}) %copy-start.2) | copy-done | bytes 147480
  39.6 2.0 %shard_map.118 = bf16[128,512]{1,0:T(8,128)(2,1)} custom-call(bf16[128,128]{1,0:T(8,128)(2,1)} %c_ref.1, bf16[144,512]{1,0:T(8,128)(2,1)} %copy-done.2, f32[128,512]{1,0:T(8,128)} %get-tuple-element.8.base_ref, f32[128,512]{1,0:T(8,128)} %get-tuple-element.9.factor_ref, f32[1,512]{1,0:T(1,128)} %bitcast.1), custom_call_target="tpu_custom_call" | custom-call | flops 1000000 | bytes 1000000 | tf_op jit(solution)/shard_map/pallas_call | solution.py:146
  (12 shorter events, 0.0 us)
Async XLA Ops:
  2.9 8.4 %copy-start.3 = (bf16[256,256]{1,0:T(8,128)(2,1)S(1)}, bf16[256,256]{1,0:T(8,128)(2,1)}, u32[]{:S(2)}) copy-start(bf16[256,256]{1,0:T(8,128)(2,1)} %get-tuple-element.6.own_ref) | copy-start | bytes 393220
  2.9 5.8 %collective-permute-start.4 = (bf16[144,512]{1,0:T(8,128)(2,1)}, bf16[144,512]{1,0:T(8,128)(2,1)S(1)}, u32[]{:S(2)}, u32[]{:S(2)}) collective-permute-start(bf16[144,512]{1,0:T(8,128)(2,1)} %get-tuple-element.7.refs_0_), channel_id=1, source_target_pairs={{0,2},{2,0},{4,6},{6,4},{8,10},{10,8},{12,14},{14,12},{1,3},{3,1},... | collective-permute-start | bytes 442376 | tf_op jit(solution)/shard_map/ppermute | solution.py:163
  8.7 0.7 %copy-start = (bf16[144,512]{1,0:T(8,128)(2,1)}, bf16[144,512]{1,0:T(8,128)(2,1)S(1)}, u32[]{:S(2)}) copy-start(bf16[144,512]{1,0:T(8,128)(2,1)S(1)} %collective-permute-done.4.refs_1_.refs_5_) | copy-start | bytes 442372
  11.1 6.3 %collective-permute-start.5 = (bf16[144,512]{1,0:T(8,128)(2,1)}, bf16[144,512]{1,0:T(8,128)(2,1)S(1)}, u32[]{:S(2)}, u32[]{:S(2)}) collective-permute-start(bf16[144,512]{1,0:T(8,128)(2,1)} %shard_map.115.refs_0_), channel_id=1, source_target_pairs={{0,4},{2,6},{4,0},{6,2},{8,12},{10,14},{12,8},{14,10},{1,5},{3,7},... | collective-permute-start | bytes 442376 | tf_op jit(solution)/shard_map/ppermute | solution.py:163
  11.3 12.6 %collective-permute-start = (bf16[256,256]{1,0:T(8,128)(2,1)S(1)}, bf16[256,256]{1,0:T(8,128)(2,1)S(1)}, u32[]{:S(2)}, u32[]{:S(2)}) collective-permute-start(bf16[256,256]{1,0:T(8,128)(2,1)S(1)} %copy-done.3), channel_id=1, source_target_pairs={{0,4},{2,6},{4,8},{6,10},{8,12},{10,14},{12,0},{14,2},{1,5},{3,7},... | collective-permute-start | bytes 393224 | tf_op jit(solution)/shard_map/ppermute | solution.py:170
  17.4 0.7 %copy-start.1 = (bf16[144,512]{1,0:T(8,128)(2,1)}, bf16[144,512]{1,0:T(8,128)(2,1)S(1)}, u32[]{:S(2)}) copy-start(bf16[144,512]{1,0:T(8,128)(2,1)S(1)} %collective-permute-done.5.refs_1_.refs_6_) | copy-start | bytes 442372
  19.8 19.1 %collective-permute-start.6 = (bf16[144,512]{1,0:T(8,128)(2,1)}, bf16[144,512]{1,0:T(8,128)(2,1)S(1)}, u32[]{:S(2)}, u32[]{:S(2)}) collective-permute-start(bf16[144,512]{1,0:T(8,128)(2,1)} %shard_map.116), channel_id=1, source_target_pairs={{0,8},{2,10},{4,12},{6,14},{8,0},{10,2},{12,4},{14,6},{1,9},{3,11}... | collective-permute-start | bytes 442376 | tf_op jit(solution)/shard_map/ppermute | solution.py:163
  22.4 6.3 %collective-permute-start.3 = (bf16[256,256]{1,0:T(8,128)(2,1)S(1)}, bf16[256,256]{1,0:T(8,128)(2,1)S(1)}, u32[]{:S(2)}, u32[]{:S(2)}) collective-permute-start(bf16[256,256]{1,0:T(8,128)(2,1)S(1)} %copy-done.3), channel_id=1, source_target_pairs={{0,2},{2,0},{4,6},{6,4},{8,10},{10,8},{12,14},{14,12},{1,3},{3,1},... | collective-permute-start | bytes 393224 | tf_op jit(solution)/shard_map/ppermute | solution.py:163
  23.9 8.3 %copy-start.4 = (bf16[256,256]{1,0:T(8,128)(2,1)}, bf16[256,256]{1,0:T(8,128)(2,1)S(1)}, u32[]{:S(2)}) copy-start(bf16[256,256]{1,0:T(8,128)(2,1)S(1)} %collective-permute-done.two_ref) | copy-start | bytes 393220
  23.9 6.2 %collective-permute-start.1 = (bf16[256,256]{1,0:T(8,128)(2,1)S(1)}, bf16[256,256]{1,0:T(8,128)(2,1)S(1)}, u32[]{:S(2)}, u32[]{:S(2)}) collective-permute-start(bf16[256,256]{1,0:T(8,128)(2,1)S(1)} %collective-permute-done.two_ref), channel_id=1, source_target_pairs={{0,2},{2,0},{4,6},{6,4},{8,10},{10,8},{12,14},{14,12},{1,3},{3,1},... | collective-permute-start | bytes 393224 | tf_op jit(solution)/shard_map/ppermute | solution.py:163
  24.4 7.7 %collective-permute-start.2 = (bf16[256,256]{1,0:T(8,128)(2,1)S(1)}, bf16[256,256]{1,0:T(8,128)(2,1)S(1)}, u32[]{:S(2)}, u32[]{:S(2)}) collective-permute-start(bf16[256,256]{1,0:T(8,128)(2,1)S(1)} %collective-permute-done.two_ref), channel_id=1, source_target_pairs={{0,0},{14,14},{2,4},{4,2},{6,8},{8,6},{10,12},{12,10},{1,1},{15,15... | collective-permute-start | bytes 393224 | tf_op jit(solution)/shard_map/ppermute | solution.py:175
  28.7 3.5 %copy-start.5 = (bf16[256,256]{1,0:T(8,128)(2,1)}, bf16[256,256]{1,0:T(8,128)(2,1)S(1)}, u32[]{:S(2)}) copy-start(bf16[256,256]{1,0:T(8,128)(2,1)S(1)} %collective-permute-done.3.pair_ref) | copy-start | bytes 393220
  30.1 2.1 %copy-start.6 = (bf16[256,256]{1,0:T(8,128)(2,1)}, bf16[256,256]{1,0:T(8,128)(2,1)S(1)}, u32[]{:S(2)}) copy-start(bf16[256,256]{1,0:T(8,128)(2,1)S(1)} %collective-permute-done.1.cross_ref) | copy-start | bytes 393220
  32.2 0.7 %copy-start.7 = (bf16[256,256]{1,0:T(8,128)(2,1)}, bf16[256,256]{1,0:T(8,128)(2,1)S(1)}, u32[]{:S(2)}) copy-start(bf16[256,256]{1,0:T(8,128)(2,1)S(1)} %collective-permute-done.2.third_ref) | copy-start | bytes 393220
  38.9 0.7 %copy-start.2 = (bf16[144,512]{1,0:T(8,128)(2,1)}, bf16[144,512]{1,0:T(8,128)(2,1)S(1)}, u32[]{:S(2)}) copy-start(bf16[144,512]{1,0:T(8,128)(2,1)S(1)} %collective-permute-done.6.state_ref) | copy-start | bytes 442372
